TPU v7x, 512 devices: a whole 4x4x16 slice. The times are simulated.
512 devices in a mesh: row: 8 (over z_hi, core), col: 16 (over y, z_lo), depth: 4 (over x).
Axes of the slice: x: 4, y: 4, z: 16 (z_hi: 4, z_lo: 4; z = z_hi * 4 + z_lo), core: 2. Of those that a mesh axis runs over, the one named last changes fastest.
Arguments:
- values: bfloat16 [768, 16, 128, 128], P(('row', 'col')), may hold values from -0.47851562 to 0.47851562
- columns: int32 [768, 16], replicated, may hold values from 0 to 767, as said below
Outputs:
- purified: bfloat16 [768, 16, 128, 128], P(('row', 'col'), 'depth')
Inputs may be any that keep to these rules, and one draw needn't show every extreme that they name: Each block row a names 16 different block columns, a itself among them, all within 8 of a around the cycle of 768 block rows (indices wrap).
All inputs are finite; a program needn't handle non-finite values.
Results may differ from a plain program's by a relative error of at most 0.0047.
Values may be sent and summed in bfloat16 or wider, within the bound.
A program may use at most 128 MiB of HBM per device.

v0:
```python
import jax
import jax.numpy as jnp
from jax import lax
from jax.sharding import PartitionSpec as P

HB = 8


def passed_along(value, axis, by):
    peers = lax.axis_size(axis)
    return lax.ppermute(value, axis, [(i, (i + by) % peers) for i in range(peers)])


def matched_blocks(nearby, band_start, own_cols, target_cols, columns):
    total_blocks = columns.shape[0]
    band_count = nearby.shape[0]
    slot_count = nearby.shape[1]
    partner_cols = jnp.take(columns, own_cols, axis=0)
    same_column = partner_cols[:, :, None, :] == target_cols[:, None, :, None]
    slot_ids = jnp.arange(slot_count, dtype=jnp.int32)
    present = jnp.any(same_column, axis=3)
    chosen = jnp.sum(jnp.where(same_column, slot_ids, 0), axis=3)
    offset = jnp.mod(own_cols - band_start, total_blocks)
    inside = offset < band_count
    usable = inside[:, :, None] & present
    flat_index = jnp.where(
        usable, offset[:, :, None] * slot_count + chosen, band_count * slot_count
    )
    flat_blocks = nearby.reshape(band_count * slot_count, nearby.shape[2], nearby.shape[3])
    return jnp.take(flat_blocks, flat_index, axis=0, mode="fill", fill_value=0)


def local(values, columns):
    own_rows, slot_count, block_size, _ = values.shape
    layers = lax.axis_size("depth")
    quarter = slot_count // layers
    layer_index = lax.axis_index("depth")
    group_index = lax.axis_index(("row", "col"))
    first_row = group_index * own_rows
    own_cols = lax.dynamic_slice_in_dim(columns, first_row, own_rows, 0)
    target_cols = lax.dynamic_slice_in_dim(own_cols, layer_index * quarter, quarter, 1)
    hop_count = (HB + own_rows - 1) // own_rows
    reach_last = HB - (hop_count - 1) * own_rows
    lower_parts = []
    upper_parts = []
    for hop_step in range(1, hop_count + 1):
        edge_rows = own_rows if hop_step < hop_count else reach_last
        from_lower = passed_along(values[own_rows - edge_rows :], ("row", "col"), hop_step)
        from_upper = passed_along(values[:edge_rows], ("row", "col"), -hop_step)
        lower_parts.insert(0, from_lower)
        upper_parts.append(from_upper)
    below_rows = jnp.concatenate(lower_parts, axis=0)
    above_rows = jnp.concatenate(upper_parts, axis=0)
    nearby = jnp.concatenate([below_rows, values, above_rows], axis=0)
    selected = matched_blocks(nearby, first_row - HB, own_cols, target_cols, columns)
    square32 = jnp.einsum("aixy,aijyz->ajxz", values, selected, preferred_element_type=jnp.float32)
    square = square32.astype(jnp.bfloat16)
    whole_square = lax.all_gather(square, "depth", axis=1, tiled=True)
    cube32 = jnp.einsum(
        "aixy,aijyz->ajxz", whole_square, selected, preferred_element_type=jnp.float32
    )
    return (3.0 * square32 - 2.0 * cube32).astype(jnp.bfloat16)


def solution(mesh):
    placed = (P(("row", "col"), None, None, None), P())
    return jax.shard_map(
        local,
        mesh=mesh,
        in_specs=placed,
        out_specs=P(("row", "col"), "depth", None, None),
        check_vma=False,
    )
```

profile of v0, /device:TPU:1, one launch (start us, length us, event | category | flops | bytes accessed | tf_op | source)
XLA Modules:
  0.0 335.9 jit_solution(13076159911926167194)
XLA Ops:
  6.5 4.6 %collective-permute-start.1 = (bf16[6,16,128,128]{3,2,1,0:T(8,128)(2,1)}, bf16[6,16,128,128]{3,2,1,0:T(8,128)(2,1)}, u32[]{:S(2)}, u32[]{:S(2)}) collective-permute-start(bf16[6,16,128,128]{3,2,1,0:T(8,128)(2,1)} %param.2), channel_id=1, source_target_pairs={{0,4},{4,8},{8,12},{12,16},{16,20},{20,24},{24,28},{28,32},{32,36}... | collective-permute-start | bytes 9437192 | tf_op jit(solution)/shard_map/ppermute | solution.py:11
  11.2 7.6 %collective-permute-start.2 = (bf16[6,16,128,128]{3,2,1,0:T(8,128)(2,1)}, bf16[6,16,128,128]{3,2,1,0:T(8,128)(2,1)}, u32[]{:S(2)}, u32[]{:S(2)}) collective-permute-start(bf16[6,16,128,128]{3,2,1,0:T(8,128)(2,1)} %param.2), channel_id=1, source_target_pairs={{0,508},{4,0},{8,4},{12,8},{16,12},{20,16},{24,20},{28,24},{32,28}... | collective-permute-start | bytes 9437192 | tf_op jit(solution)/shard_map/ppermute | solution.py:11
  18.8 3.2 fusion.18
  22.0 1.9 collective-permute-start
  23.9 6.7 %collective-permute-start.3 = (bf16[2,16,128,128]{3,2,1,0:T(8,128)(2,1)}, bf16[2,16,128,128]{3,2,1,0:T(8,128)(2,1)}, u32[]{:S(2)}, u32[]{:S(2)}) collective-permute-start(bf16[2,16,128,128]{3,2,1,0:T(8,128)(2,1)} %get-tuple-element.7), channel_id=1, source_target_pairs={{0,504},{4,508},{8,0},{12,4},{16,8},{20,12},{24,16},{28,20},{32,24... | collective-permute-start | bytes 3145736 | tf_op jit(solution)/shard_map/ppermute | solution.py:11
  30.6 1.0 copy.39
  31.5 0.5 compare_and_fusion.1
  32.1 0.6 reshape.50
  32.7 0.7 pad_clamp_fusion.1
  33.3 1.4 dynamic_slice.7
  34.7 0.8 copy.41
  35.5 1.2 gather_fusion
  36.7 0.9 broadcast_select_fusion.7
  37.6 0.6 compare_reduce_fusion
  38.1 0.6 fusion.14
  38.7 0.1 copy.43
  38.9 0.1 reshape.58
  39.0 0.1 copy.42
  39.1 138.4 %collective-permute-done = bf16[2,16,128,128]{3,2,1,0:T(8,128)(2,1)} collective-permute-done((bf16[2,16,128,128]{3,2,1,0:T(8,128)(2,1)}, bf16[2,16,128,128]{3,2,1,0:T(8,128)(2,1)}, u32[]{:S(2)}, u32[]{:S(2)}) %collective-permute-start) | collective-permute-done | bytes 1048608 | tf_op jit(solution)/shard_map/ppermute | solution.py:11
  177.5 2.4 constant_dynamic-update-slice_fusion.4
  179.8 3.9 %constant_dynamic-update-slice_fusion.3 = bf16[22,16,128,128]{3,2,1,0:T(8,128)(2,1)} fusion(bf16[22,16,128,128]{3,2,1,0:T(8,128)(2,1)} %constant_dynamic-update-slice_fusion.4, bf16[6,16,128,128]{3,2,1,0:T(8,128)(2,1)} %collective-permute-done.1), kind=kLoop, calls=%fused_computation.30 | loop fusion | bytes 6291456
  183.8 2.1 constant_dynamic-update-slice_fusion.2
  185.9 4.0 %constant_dynamic-update-slice_fusion.1 = bf16[22,16,128,128]{3,2,1,0:T(8,128)(2,1)} fusion(bf16[22,16,128,128]{3,2,1,0:T(8,128)(2,1)} %constant_dynamic-update-slice_fusion.2, bf16[6,16,128,128]{3,2,1,0:T(8,128)(2,1)} %collective-permute-done.2), kind=kLoop, calls=%fused_computation.28 | loop fusion | bytes 6291456
  189.8 50.2 %collective-permute-done.3 = bf16[2,16,128,128]{3,2,1,0:T(8,128)(2,1)} collective-permute-done((bf16[2,16,128,128]{3,2,1,0:T(8,128)(2,1)}, bf16[2,16,128,128]{3,2,1,0:T(8,128)(2,1)}, u32[]{:S(2)}, u32[]{:S(2)}) %collective-permute-start.3) | collective-permute-done | bytes 1048608 | tf_op jit(solution)/shard_map/ppermute | solution.py:11
  240.1 2.3 constant_dynamic-update-slice_fusion
  242.4 15.5 %gather_fusion.1 = bf16[384,128,128]{2,1,0:T(8,128)(2,1)} fusion(bf16[352,128,128]{2,1,0:T(8,128)(2,1)} %bitcast.1, s32[1024]{0:T(1024)S(1)} %pad_clamp_fusion), kind=kCustom, calls=%fused_computation.1 | custom fusion | bytes 25167360 | tf_op jit(solution)/shard_map/jit(_take)/gather | solution.py:30
  257.9 7.9 %fusion = f32[6,4,128,128,1]{3,2,1,4,0:T(8,128)S(1)} fusion(bf16[6,16,4,128,128]{4,3,2,1,0:T(8,128)(2,1)} %bitcast.62, pred[6,16,4]{2,1,0:T(8,128)(4,1)S(1)} %copy.42, bf16[6,16,128,128]{3,2,1,0:T(8,128)(2,1)S(1)} %copy-done), kind=kOutput, calls=%fused_computation.3 | convolution fusion | flops 1616904192 | bytes 17301888 | tf_op jit(solution)/shard_map/aixy,aijyz->ajxz/dot_general | solution.py:56
  265.8 1.1 copy-done.1
  266.9 1.0 fusion.13
  268.0 51.1 %all-gather.2.cloned.1.call-done = bf16[6,16,128,128]{2,3,1,0:T(8,128)(2,1)} async-done(((bf16[6,4,128,128]{2,3,1,0:T(8,128)(2,1)}), bf16[6,16,128,128]{2,3,1,0:T(8,128)(2,1)}) %all-gather.2.cloned.1.call-update) | async-done | bytes 3145744 | tf_op jit(solution)/shard_map/all_gather | solution.py:58
  319.1 8.7 %fusion.10 = bf16[6,4,128,128]{2,3,1,0:T(8,128)(2,1)S(1)} fusion(bf16[6,16,128,128]{2,3,1,0:T(8,128)(2,1)} %all-gather.2.cloned.1.call-done, bf16[6,16,4,128,128]{4,3,2,1,0:T(8,128)(2,1)} %bitcast.63, pred[6,16,4]{2,1,0:T(8,128)(4,1)S(1)} %copy.42, f32[6,4,128,128,1]{3,2,1,4,0:T(8,128)} %copy-done.1), kind=kOutput, calls=%fused_computation.14 | convolution fusion | flops 1618477056 | bytes 18088320 | tf_op jit(solution)/shard_map/aixy,aijyz->ajxz/dot_general | solution.py:59
  327.9 1.2 copy.47
  (11 shorter events, 0.1 us)
Async XLA Ops:
  6.5 177.3 %copy-start = (bf16[6,16,128,128]{3,2,1,0:T(8,128)(2,1)S(1)}, bf16[6,16,128,128]{3,2,1,0:T(8,128)(2,1)}, u32[]{:S(2)}) copy-start(bf16[6,16,128,128]{3,2,1,0:T(8,128)(2,1)} %param.2) | copy-start | bytes 9437188
  6.5 312.6 %all-gather.2.cloned.1.call-start = ((), (), s32[]{:S(2)}) async-start(), calls=%async_computation | async-start | bytes 3932160 | tf_op jit(solution)/shard_map/all_gather | solution.py:58
  6.5 173.3 %collective-permute-start.1 = (bf16[6,16,128,128]{3,2,1,0:T(8,128)(2,1)}, bf16[6,16,128,128]{3,2,1,0:T(8,128)(2,1)}, u32[]{:S(2)}, u32[]{:S(2)}) collective-permute-start(bf16[6,16,128,128]{3,2,1,0:T(8,128)(2,1)} %param.2), channel_id=1, source_target_pairs={{0,4},{4,8},{8,12},{12,16},{16,20},{20,24},{24,28},{28,32},{32,36}... | collective-permute-start | bytes 9437192 | tf_op jit(solution)/shard_map/ppermute | solution.py:11
  11.2 174.7 %collective-permute-start.2 = (bf16[6,16,128,128]{3,2,1,0:T(8,128)(2,1)}, bf16[6,16,128,128]{3,2,1,0:T(8,128)(2,1)}, u32[]{:S(2)}, u32[]{:S(2)}) collective-permute-start(bf16[6,16,128,128]{3,2,1,0:T(8,128)(2,1)} %param.2), channel_id=1, source_target_pairs={{0,508},{4,0},{8,4},{12,8},{16,12},{20,16},{24,20},{28,24},{32,28}... | collective-permute-start | bytes 9437192 | tf_op jit(solution)/shard_map/ppermute | solution.py:11
  22.0 155.5 %collective-permute-start = (bf16[2,16,128,128]{3,2,1,0:T(8,128)(2,1)}, bf16[2,16,128,128]{3,2,1,0:T(8,128)(2,1)}, u32[]{:S(2)}, u32[]{:S(2)}) collective-permute-start(bf16[2,16,128,128]{3,2,1,0:T(8,128)(2,1)} %get-tuple-element.8), channel_id=1, source_target_pairs={{0,8},{4,12},{8,16},{12,20},{16,24},{20,28},{24,32},{28,36},{32,40... | collective-permute-start | bytes 3145736 | tf_op jit(solution)/shard_map/ppermute | solution.py:11
  23.9 216.2 %collective-permute-start.3 = (bf16[2,16,128,128]{3,2,1,0:T(8,128)(2,1)}, bf16[2,16,128,128]{3,2,1,0:T(8,128)(2,1)}, u32[]{:S(2)}, u32[]{:S(2)}) collective-permute-start(bf16[2,16,128,128]{3,2,1,0:T(8,128)(2,1)} %get-tuple-element.7), channel_id=1, source_target_pairs={{0,504},{4,508},{8,0},{12,4},{16,8},{20,12},{24,16},{28,20},{32,24... | collective-permute-start | bytes 3145736 | tf_op jit(solution)/shard_map/ppermute | solution.py:11
  265.8 1.1 copy-start.1
Sparse Core Ops, SparseCore 0:
  268.1 50.9 all-gather.1
where the time goes:
time: 336 us
  waiting for transfers between devices  240 us (71%)
  local copies, waits for them, and re-layouts  40.9 us (12%)
  starting transfers between devices  20.8 us (6%)
  matrix products  16.6 us (5%)
  between operations  13.5 us (4%)
  other arithmetic  4.28 us (1%)
    ppermute x4, waiting for transfers between devices, passed_along(): lax.ppermute(value, axis, [(i, (i + by) % peers) for i in range(peers)])  189 us
    all_gather x1, waiting for transfers between devices, local(): whole_square = lax.all_gather(square, 'depth', axis=1, tiled=True)  51.1 us
    ppermute x4, starting transfers between devices, passed_along(): lax.ppermute(value, axis, [(i, (i + by) % peers) for i in range(peers)])  20.8 us
    gather x1, local copies, waits for them, and re-layouts, matched_blocks(): return jnp.take(flat_blocks, flat_index, axis=0, mode='fill', fill_value=0)  15.5 us
    unnamed x9, local copies, waits for them, and re-layouts  14.4 us
    dot_general x1, matrix products, local(): jnp.einsum('aixy,aijyz->ajxz', whole_square, selected, preferred_element_...  8.72 us
    dot_general x1, matrix products, local(): jnp.einsum('aixy,aijyz->ajxz', values, selected, preferred_element_type=j...  7.87 us
  transfers between devices with their start and end apart: 5, of which 3 were waited for; matrix products, arithmetic and copies ran while one was open for 7% of the time, Pallas kernels for 0%

commit v1 on v0

--- a/solution.py
+++ b/solution.py
@@ -4,6 +4,22 @@
 from jax.sharding import PartitionSpec as P
 
 HB = 8
+
+
+def product_in_turn(x, axis, dim, product):
+    length, here, rows = (lax.axis_size(axis), lax.axis_index(axis), x.shape[dim])
+    upward = [(i, (i + 1) % length) for i in range(length)]
+    backward = [(i, (i - 1) % length) for i in range(length)]
+    middle = length // 2
+    from_left = from_right = x
+    running = product(x, here * rows)
+    for lap in range(1, middle + 1):
+        from_left = lax.ppermute(from_left, axis, upward)
+        if lap < length - middle:
+            from_right = lax.ppermute(from_right, axis, backward)
+            running = running + product(from_right, (here + lap) % length * rows)
+        running = running + product(from_left, (here - lap) % length * rows)
+    return running
 
 
 def passed_along(value, axis, by):
@@ -55,9 +71,16 @@
     selected = matched_blocks(nearby, first_row - HB, own_cols, target_cols, columns)
     square32 = jnp.einsum("aixy,aijyz->ajxz", values, selected, preferred_element_type=jnp.float32)
     square = square32.astype(jnp.bfloat16)
-    whole_square = lax.all_gather(square, "depth", axis=1, tiled=True)
-    cube32 = jnp.einsum(
-        "aixy,aijyz->ajxz", whole_square, selected, preferred_element_type=jnp.float32
+    cube32 = product_in_turn(
+        square,
+        "depth",
+        1,
+        lambda shard, offset_2: jnp.einsum(
+            "aixy,aijyz->ajxz",
+            shard,
+            lax.dynamic_slice_in_dim(selected, offset_2, shard.shape[1], axis=1),
+            preferred_element_type=jnp.float32,
+        ),
     )
     return (3.0 * square32 - 2.0 * cube32).astype(jnp.bfloat16)
 

time: 336 us -> 329 us (0.979)
  waiting for transfers between devices: 240 us -> 216 us
  local copies, waits for them, and re-layouts: 40.9 us -> 54.5 us
  between operations: 13.5 us -> 0.26 us
  starting transfers between devices: 20.8 us -> 29 us
  other arithmetic: 4.28 us -> 9.78 us
    all_gather x1 -> x0, waiting for transfers between devices: 51.1 us -> none  [local(): whole_square = lax.all_gather(square, 'depth', axis=1, tiled=True)]
    ppermute x0 -> x3, waiting for transfers between devices: none -> 25.3 us  [the longest x2 25.3 us: product_in_turn(): from_left = lax.ppermute(from_left, axis, upward)]
    gather x1 -> x2, local copies, waits for them, and re-layouts: 15.5 us -> 32.2 us  [matched_blocks(): return jnp.take(flat_blocks, flat_index, axis=0, mode='fill', fill_value=0)]
    ppermute x0 -> x3, starting transfers between devices: none -> 8.4 us  [the longest x2 4.97 us: product_in_turn(): from_left = lax.ppermute(from_left, axis, upward)]
    select_n x1 -> x2, other arithmetic: 0.02 us -> 6.34 us  [matched_blocks(): return jnp.take(flat_blocks, flat_index, axis=0, mode='fill', fill_value=0)]
    unnamed x9 -> x11, local copies, waits for them, and re-layouts: 14.4 us -> 11.4 us
    dot_general x1 -> x4, matrix products: 8.72 us -> 9.73 us  [local(): jnp.einsum('aixy,aijyz->ajxz', shard, lax.dynamic_slice_in_dim(selected,...]
  transfers between devices with their start and end apart: 5 -> 7, of which waited for: 3 -> 4; matrix products, arithmetic and copies ran while one was open for 7% -> 9% of each run, Pallas kernels for 0% -> 0%
where the time goes in v1:
time: 329 us; the launch traced here: 327 us
  waiting for transfers between devices  216 us (66%)
  local copies, waits for them, and re-layouts  54.5 us (17%)
  starting transfers between devices  29 us (9%)
  matrix products  17.4 us (5%)
  other arithmetic  9.78 us (3%)
    ppermute x4, waiting for transfers between devices, passed_along(): lax.ppermute(value, axis, [(i, (i + by) % peers) for i in range(peers)])  191 us
    gather x2, local copies, waits for them, and re-layouts, matched_blocks(): return jnp.take(flat_blocks, flat_index, axis=0, mode='fill', fill_value=0)  32.2 us
    ppermute x2, waiting for transfers between devices, product_in_turn(): from_left = lax.ppermute(from_left, axis, upward)  25.3 us
    ppermute x4, starting transfers between devices, passed_along(): lax.ppermute(value, axis, [(i, (i + by) % peers) for i in range(peers)])  20.6 us
    unnamed x11, local copies, waits for them, and re-layouts  11.4 us
    dot_general x4, matrix products, local(): jnp.einsum('aixy,aijyz->ajxz', shard, lax.dynamic_slice_in_dim(selected,...  9.73 us
    dot_general x1, matrix products, local(): jnp.einsum('aixy,aijyz->ajxz', values, selected, preferred_element_type=j...  7.64 us
  transfers between devices with their start and end apart: 7, of which 4 were waited for; matrix products, arithmetic and copies ran while one was open for 9% of the time, Pallas kernels for 0%

profile of v1, /device:TPU:1, one launch (start us, length us, event | category | flops | bytes accessed | tf_op | source)
XLA Modules:
  0.0 326.7 jit_solution(7080814978515853620)
XLA Ops:
  0.0 4.4 %collective-permute-start.1 = (bf16[6,16,128,128]{3,2,1,0:T(8,128)(2,1)}, bf16[6,16,128,128]{3,2,1,0:T(8,128)(2,1)}, u32[]{:S(2)}, u32[]{:S(2)}) collective-permute-start(bf16[6,16,128,128]{3,2,1,0:T(8,128)(2,1)} %param.2), channel_id=1, source_target_pairs={{0,4},{4,8},{8,12},{12,16},{16,20},{20,24},{24,28},{28,32},{32,36}... | collective-permute-start | bytes 9437192 | tf_op jit(solution)/shard_map/ppermute | solution.py:27
  4.4 7.6 %collective-permute-start.2 = (bf16[6,16,128,128]{3,2,1,0:T(8,128)(2,1)}, bf16[6,16,128,128]{3,2,1,0:T(8,128)(2,1)S(1)}, u32[]{:S(2)}, u32[]{:S(2)}) collective-permute-start(bf16[6,16,128,128]{3,2,1,0:T(8,128)(2,1)} %param.2), channel_id=1, source_target_pairs={{0,508},{4,0},{8,4},{12,8},{16,12},{20,16},{24,20},{28,24},{32,28}... | collective-permute-start | bytes 9437192 | tf_op jit(solution)/shard_map/ppermute | solution.py:27
  12.0 3.2 fusion.29
  15.2 1.9 collective-permute-start
  17.1 6.7 %collective-permute-start.3 = (bf16[2,16,128,128]{3,2,1,0:T(8,128)(2,1)}, bf16[2,16,128,128]{3,2,1,0:T(8,128)(2,1)}, u32[]{:S(2)}, u32[]{:S(2)}) collective-permute-start(bf16[2,16,128,128]{3,2,1,0:T(8,128)(2,1)} %get-tuple-element.7), channel_id=1, source_target_pairs={{0,504},{4,508},{8,0},{12,4},{16,8},{20,12},{24,16},{28,20},{32,24... | collective-permute-start | bytes 3145736 | tf_op jit(solution)/shard_map/ppermute | solution.py:27
  23.8 1.0 copy.46
  25.9 0.7 pad_clamp_fusion.1
  26.6 1.4 dynamic_slice.19
  28.0 0.8 copy.48
  28.7 1.2 gather_fusion
  29.9 0.9 broadcast_select_fusion.1
  32.3 138.4 %collective-permute-done = bf16[2,16,128,128]{3,2,1,0:T(8,128)(2,1)} collective-permute-done((bf16[2,16,128,128]{3,2,1,0:T(8,128)(2,1)}, bf16[2,16,128,128]{3,2,1,0:T(8,128)(2,1)}, u32[]{:S(2)}, u32[]{:S(2)}) %collective-permute-start) | collective-permute-done | bytes 1048608 | tf_op jit(solution)/shard_map/ppermute | solution.py:27
  170.7 2.4 constant_dynamic-update-slice_fusion.4
  173.1 4.1 %constant_dynamic-update-slice_fusion.3 = bf16[22,16,128,128]{3,2,1,0:T(8,128)(2,1)} fusion(bf16[22,16,128,128]{3,2,1,0:T(8,128)(2,1)} %constant_dynamic-update-slice_fusion.4, bf16[6,16,128,128]{3,2,1,0:T(8,128)(2,1)} %collective-permute-done.1), kind=kLoop, calls=%fused_computation.41 | loop fusion | bytes 6291456
  177.2 2.1 constant_dynamic-update-slice_fusion.2
  179.2 1.9 constant_dynamic-update-slice_fusion.1
  181.1 52.1 %collective-permute-done.3 = bf16[2,16,128,128]{3,2,1,0:T(8,128)(2,1)} collective-permute-done((bf16[2,16,128,128]{3,2,1,0:T(8,128)(2,1)}, bf16[2,16,128,128]{3,2,1,0:T(8,128)(2,1)}, u32[]{:S(2)}, u32[]{:S(2)}) %collective-permute-start.3) | collective-permute-done | bytes 1048608 | tf_op jit(solution)/shard_map/ppermute | solution.py:27
  233.3 2.3 constant_dynamic-update-slice_fusion
  235.6 15.5 %gather_fusion.1 = bf16[384,128,128]{2,1,0:T(8,128)(2,1)} fusion(bf16[352,128,128]{2,1,0:T(8,128)(2,1)} %bitcast.1, s32[1024]{0:T(1024)S(1)} %pad_clamp_fusion), kind=kCustom, calls=%fused_computation.1 | custom fusion | bytes 25167360 | tf_op jit(solution)/shard_map/jit(_take)/gather | solution.py:46
  251.1 16.7 %copy.50 = bf16[6,16,4,128,128]{3,4,1,2,0:T(8,128)(2,1)} copy(bf16[6,16,4,128,128]{4,3,2,1,0:T(8,128)(2,1)} %bitcast.91) | data formatting | bytes 25165824 | tf_op jit(solution)/shard_map/jit(_take)/gather | solution.py:46
  267.9 6.3 %broadcast_select_fusion = bf16[6,16,4,128,128]{3,4,1,2,0:T(8,128)(2,1)S(1)} fusion(bf16[6,16,4,128,128]{3,4,1,2,0:T(8,128)(2,1)} %copy.50, pred[6,16,4]{1,2,0:T(4,128)(4,1)S(1)} %compare_and_fusion), kind=kLoop, calls=%fused_computation.2 | loop fusion | flops 6291456 | bytes 25166208 | tf_op jit(solution)/shard_map/jit(_take)/select_n | solution.py:46
  274.2 7.6 %fusion = f32[6,4,128,128,1]{3,2,4,1,0:T(8,128)S(1)} fusion(bf16[6,16,4,128,128]{3,4,1,2,0:T(8,128)(2,1)S(1)} %broadcast_select_fusion, bf16[6,16,128,128]{3,2,1,0:T(8,128)(2,1)} %param.2), kind=kOutput, calls=%fused_computation.3 | convolution fusion | flops 1610612736 | bytes 17301504 | tf_op jit(solution)/shard_map/aixy,aijyz->ajxz/dot_general | solution.py:72
  282.0 3.1 collective-permute-start.5
  285.1 3.4 %collective-permute-start.4 = (bf16[6,4,128,128]{2,3,1,0:T(8,128)(2,1)S(1)}, bf16[6,4,128,128]{2,3,1,0:T(8,128)(2,1)}, u32[]{:S(2)}, u32[]{:S(2)}) collective-permute-start(bf16[6,4,128,128]{2,3,1,0:T(8,128)(2,1)S(1)} %fusion.22), channel_id=1, source_target_pairs={{0,3},{1,0},{2,1},{3,2},{4,7},{5,4},{6,5},{7,6},{8,11},{9,8},{10,9... | collective-permute-start | bytes 2359304 | tf_op jit(solution)/shard_map/ppermute | solution.py:19
  288.6 15.2 %collective-permute-done.5 = bf16[6,4,128,128]{2,3,1,0:T(8,128)(2,1)S(1)} collective-permute-done((bf16[6,4,128,128]{2,3,1,0:T(8,128)(2,1)S(1)}, bf16[6,4,128,128]{2,3,1,0:T(8,128)(2,1)S(1)}, u32[]{:S(2)}, u32[]{:S(2)}) %collective-permute-start.5) | collective-permute-done | bytes 786464 | tf_op jit(solution)/shard_map/ppermute | solution.py:17
  303.7 1.9 collective-permute-start.6
  305.6 3.0 fusion.8
  308.7 3.5 %fusion.4 = f32[6,4,128,128,1]{3,2,4,1,0:T(8,128)S(1)} fusion(bf16[6,16,4,128,128]{3,4,1,2,0:T(8,128)(2,1)} %copy-done, s32[]{:T(128)S(6)} %select_n.109, bf16[6,4,128,128]{2,3,1,0:T(8,128)(2,1)S(1)} %collective-permute-done.5), kind=kOutput, calls=%fused_computation.7 | convolution fusion | flops 402653184 | bytes 5505028 | tf_op jit(solution)/shard_map/aixy,aijyz->ajxz/dot_general | solution.py:78
  312.2 2.1 fusion.6
  314.3 10.2 %collective-permute-done.6 = bf16[6,4,128,128]{2,3,1,0:T(8,128)(2,1)S(1)} collective-permute-done((bf16[6,4,128,128]{2,3,1,0:T(8,128)(2,1)S(1)}, bf16[6,4,128,128]{2,3,1,0:T(8,128)(2,1)S(1)}, u32[]{:S(2)}, u32[]{:S(2)}) %collective-permute-start.6) | collective-permute-done | bytes 786464 | tf_op jit(solution)/shard_map/ppermute | solution.py:17
  324.5 1.1 fusion.15
  325.6 1.2 copy.55
  (20 shorter events, 2.7 us)
Async XLA Ops:
  0.0 173.1 %collective-permute-start.1 = (bf16[6,16,128,128]{3,2,1,0:T(8,128)(2,1)}, bf16[6,16,128,128]{3,2,1,0:T(8,128)(2,1)}, u32[]{:S(2)}, u32[]{:S(2)}) collective-permute-start(bf16[6,16,128,128]{3,2,1,0:T(8,128)(2,1)} %param.2), channel_id=1, source_target_pairs={{0,4},{4,8},{8,12},{12,16},{16,20},{20,24},{24,28},{28,32},{32,36}... | collective-permute-start | bytes 9437192 | tf_op jit(solution)/shard_map/ppermute | solution.py:27
  4.4 174.8 %collective-permute-start.2 = (bf16[6,16,128,128]{3,2,1,0:T(8,128)(2,1)}, bf16[6,16,128,128]{3,2,1,0:T(8,128)(2,1)S(1)}, u32[]{:S(2)}, u32[]{:S(2)}) collective-permute-start(bf16[6,16,128,128]{3,2,1,0:T(8,128)(2,1)} %param.2), channel_id=1, source_target_pairs={{0,508},{4,0},{8,4},{12,8},{16,12},{20,16},{24,20},{28,24},{32,28}... | collective-permute-start | bytes 9437192 | tf_op jit(solution)/shard_map/ppermute | solution.py:27
  15.2 155.5 %collective-permute-start = (bf16[2,16,128,128]{3,2,1,0:T(8,128)(2,1)}, bf16[2,16,128,128]{3,2,1,0:T(8,128)(2,1)}, u32[]{:S(2)}, u32[]{:S(2)}) collective-permute-start(bf16[2,16,128,128]{3,2,1,0:T(8,128)(2,1)} %get-tuple-element.8), channel_id=1, source_target_pairs={{0,8},{4,12},{8,16},{12,20},{16,24},{20,28},{24,32},{28,36},{32,40... | collective-permute-start | bytes 3145736 | tf_op jit(solution)/shard_map/ppermute | solution.py:27
  17.1 216.2 %collective-permute-start.3 = (bf16[2,16,128,128]{3,2,1,0:T(8,128)(2,1)}, bf16[2,16,128,128]{3,2,1,0:T(8,128)(2,1)}, u32[]{:S(2)}, u32[]{:S(2)}) collective-permute-start(bf16[2,16,128,128]{3,2,1,0:T(8,128)(2,1)} %get-tuple-element.7), channel_id=1, source_target_pairs={{0,504},{4,508},{8,0},{12,4},{16,8},{20,12},{24,16},{28,20},{32,24... | collective-permute-start | bytes 3145736 | tf_op jit(solution)/shard_map/ppermute | solution.py:27
  173.1 4.1 %copy-start.2 = (bf16[6,16,128,128]{3,2,1,0:T(8,128)(2,1)S(1)}, bf16[6,16,128,128]{3,2,1,0:T(8,128)(2,1)}, u32[]{:S(2)}) copy-start(bf16[6,16,128,128]{3,2,1,0:T(8,128)(2,1)} %param.2) | copy-start | bytes 9437188
  274.2 7.7 %copy-start = (bf16[6,16,4,128,128]{3,4,1,2,0:T(8,128)(2,1)}, bf16[6,16,4,128,128]{3,4,1,2,0:T(8,128)(2,1)S(1)}, u32[]{:S(2)}) copy-start(bf16[6,16,4,128,128]{3,4,1,2,0:T(8,128)(2,1)S(1)} %broadcast_select_fusion) | copy-start | bytes 37748740
  282.0 21.7 %collective-permute-start.5 = (bf16[6,4,128,128]{2,3,1,0:T(8,128)(2,1)S(1)}, bf16[6,4,128,128]{2,3,1,0:T(8,128)(2,1)S(1)}, u32[]{:S(2)}, u32[]{:S(2)}) collective-permute-start(bf16[6,4,128,128]{2,3,1,0:T(8,128)(2,1)S(1)} %fusion.22), channel_id=1, source_target_pairs={{0,1},{1,2},{2,3},{3,0},{4,5},{5,6},{6,7},{7,4},{8,9},{9,10},{10,1... | collective-permute-start | bytes 2359304 | tf_op jit(solution)/shard_map/ppermute | solution.py:17
  285.1 27.2 %collective-permute-start.4 = (bf16[6,4,128,128]{2,3,1,0:T(8,128)(2,1)S(1)}, bf16[6,4,128,128]{2,3,1,0:T(8,128)(2,1)}, u32[]{:S(2)}, u32[]{:S(2)}) collective-permute-start(bf16[6,4,128,128]{2,3,1,0:T(8,128)(2,1)S(1)} %fusion.22), channel_id=1, source_target_pairs={{0,3},{1,0},{2,1},{3,2},{4,7},{5,4},{6,5},{7,6},{8,11},{9,8},{10,9... | collective-permute-start | bytes 2359304 | tf_op jit(solution)/shard_map/ppermute | solution.py:19
  303.7 20.8 %collective-permute-start.6 = (bf16[6,4,128,128]{2,3,1,0:T(8,128)(2,1)S(1)}, bf16[6,4,128,128]{2,3,1,0:T(8,128)(2,1)S(1)}, u32[]{:S(2)}, u32[]{:S(2)}) collective-permute-start(bf16[6,4,128,128]{2,3,1,0:T(8,128)(2,1)S(1)} %collective-permute-done.5), channel_id=1, source_target_pairs={{0,1},{1,2},{2,3},{3,0},{4,5},{5,6},{6,7},{7,4},{8,9},{9,10},{10,1... | collective-permute-start | bytes 2359304 | tf_op jit(solution)/shard_map/ppermute | solution.py:17
  305.6 6.6 %copy-start.1 = (bf16[6,16,4,128,128]{3,4,1,2,0:T(8,128)(2,1)S(1)}, bf16[6,16,4,128,128]{3,4,1,2,0:T(8,128)(2,1)}, u32[]{:S(2)}) copy-start(bf16[6,16,4,128,128]{3,4,1,2,0:T(8,128)(2,1)} %copy-done) | copy-start | bytes 37748740
